TPU v7x, 32 devices: a whole 2x2x4 slice. The times are simulated.
32 devices in a mesh: section: 4 (over y, x), scen: 8 (over z, core).
Axes of the slice: x: 2, y: 2, z: 4, core: 2. Of those that a mesh axis runs over, the one named last changes fastest.
Arguments:
- right_side: float32 [4, 8, 512, 1024], P('section', 'scen'), may hold values from -6 to 6
- inverse_raw: bfloat16 [4, 8, 1024, 1024], P('section', 'scen'), may hold values from -0.1875 to 0.1875
- inverse_pattern: int32 [4, 8, 16, 16], P('section', 'scen'), may hold values 0 or 1
- coupling: bfloat16 [4, 8, 1024, 1024], P('section', 'scen'), may hold values from -0.1875 to 0.1875
- coupling_pattern: int32 [4, 8, 16, 16], P('section', 'scen'), may hold values 0 or 1
- pivots: float32 [4, 8, 1024], P('section', 'scen'), may hold values from 0.5 to 2
- offsets: int32 [4, 8], replicated, may hold values from 0 to 1, as said below
- above_solution: bfloat16 [8, 512, 1024], P('scen'), may hold values from -6 to 6
Outputs:
- solution: float32 [4, 8, 512, 1024], P('section', 'scen')
Inputs may be any that keep to these rules, and one draw needn't show every extreme that they name: Node c of level l has node c + offsets[l, c] of level l - 1 as its parent, and for l = 0 row c + offsets[0, c] of above_solution; offsets[l, 0] is 1 and offsets[l, 7] is 0 for every l.
All inputs are finite; a program needn't handle non-finite values. No bound on the sum of `inverse_pattern` or of `coupling_pattern` on one device may be relied on, other than what follows from the above.
Results may differ from a plain program's by a relative error of at most 0.0075.
Values may be sent and summed in bfloat16 or wider, within the bound.
A program may use at most 64 MiB of HBM per device.

v0:
```python
import jax
import jax.numpy as jnp
from jax import lax
from jax.sharding import PartitionSpec as P

PANEL = 64


def shifted(array, axis, by):
    length = lax.axis_size(axis)
    pairs = [(i, i + by) for i in range(length) if 0 <= i + by < length]
    return lax.ppermute(array, axis, pairs)


def times_transposed(left_rows, matrix):
    return lax.dot_general(
        left_rows, matrix, (((1,), (1,)), ((), ())), preferred_element_type=jnp.float32
    )


def widen_pattern(pattern, block_size):
    return jnp.repeat(jnp.repeat(pattern, block_size, axis=0), block_size, axis=1)


def unit_inverse(raw_values, pattern):
    features = raw_values.shape[0]
    widened = widen_pattern(pattern, features // pattern.shape[0])
    row_ids = lax.broadcasted_iota(jnp.int32, (features, features), 0)
    col_ids = lax.broadcasted_iota(jnp.int32, (features, features), 1)
    kept_mask = (widened > 0) & (row_ids > col_ids)
    unit_part = jnp.where(row_ids == col_ids, jnp.ones_like(raw_values), jnp.zeros_like(raw_values))
    return jnp.where(kept_mask, raw_values, unit_part)


def masked_coupling(raw_values, pattern):
    widened = widen_pattern(pattern, raw_values.shape[0] // pattern.shape[0])
    return jnp.where(widened > 0, raw_values, jnp.zeros_like(raw_values))


def local(
    right_side,
    inverse_raw,
    inverse_pattern,
    coupling,
    coupling_pattern,
    pivots,
    offsets,
    above_solution,
):
    section_index = lax.axis_index("section")
    levels = lax.axis_size("section")
    node_index = lax.axis_index("scen")
    factor = unit_inverse(inverse_raw[0, 0], inverse_pattern[0, 0])
    linking = masked_coupling(coupling[0, 0], coupling_pattern[0, 0])
    pivot_row = pivots[0, 0]
    given = right_side[0, 0]
    above_rows = above_solution[0]
    total_rows, features = given.shape
    child_level = jnp.minimum(section_index + 1, levels - 1)
    child_here = offsets[child_level, node_index]
    child_left = offsets[child_level, jnp.maximum(node_index - 1, 0)]
    own_offset = offsets[section_index, node_index]
    piece_rows = PANEL
    pieces = total_rows // piece_rows
    empty_half = jnp.zeros((piece_rows, features), jnp.bfloat16)

    def forward_step(step_index, incoming, kept_w):
        piece = step_index - (levels - 1 - section_index)
        active_now = (piece >= 0) & (piece < pieces)
        first_row = jnp.clip(piece, 0, pieces - 1) * piece_rows

        def forward_compute():
            given_rows = lax.dynamic_slice_in_dim(given, first_row, piece_rows, 0)
            reduced = (given_rows - incoming).astype(jnp.bfloat16)
            forward_rows = times_transposed(reduced, factor)
            kept = lax.dynamic_update_slice_in_dim(
                kept_w, forward_rows * pivot_row[None, :], first_row, 0
            )
            child_term = lax.cond(
                section_index > 0,
                lambda: times_transposed(forward_rows.astype(jnp.bfloat16), linking).astype(
                    jnp.bfloat16
                ),
                lambda: empty_half,
            )
            return (child_term, kept)

        def forward_resting():
            return (empty_half, kept_w)

        child_term, kept_w = lax.cond(active_now, forward_compute, forward_resting)
        upward = shifted(child_term, "section", -1)
        beside = shifted(upward, "scen", 1)
        incoming = jnp.where(child_here == 0, upward.astype(jnp.float32), 0.0) + jnp.where(
            child_left == 1, beside.astype(jnp.float32), 0.0
        )
        return (incoming, kept_w)

    def above_piece(source, index):
        return lax.dynamic_slice_in_dim(
            source, jnp.clip(index, 0, pieces - 1) * piece_rows, piece_rows, 0
        )

    def backward_step(step_index, parent_base, parent_side, kept_w, solved):
        piece = step_index - section_index
        active_now = (piece >= 0) & (piece < pieces)
        first_row = jnp.clip(piece, 0, pieces - 1) * piece_rows
        beside = shifted(parent_base, "scen", -1)
        parent_rows = jnp.where(own_offset == 1, beside, parent_base)

        def backward_compute():
            kept_rows = lax.dynamic_slice_in_dim(kept_w, first_row, piece_rows, 0)
            reduced = kept_rows - jnp.dot(parent_rows, linking, preferred_element_type=jnp.float32)
            solution_rows = jnp.dot(
                reduced.astype(jnp.bfloat16), factor, preferred_element_type=jnp.float32
            )
            return (
                solution_rows.astype(jnp.bfloat16),
                lax.dynamic_update_slice_in_dim(solved, solution_rows, first_row, 0),
            )

        def backward_resting():
            return (empty_half, solved)

        sent, solved = lax.cond(active_now, backward_compute, backward_resting)
        received = shifted(sent, "section", 1)
        parent_base = jnp.where(
            section_index == 0, above_piece(above_rows, step_index + 1), received
        )
        parent_side = empty_half
        return (parent_base, parent_side, solved)

    incoming = jnp.zeros((piece_rows, features), jnp.float32)
    kept_w = jnp.zeros((total_rows, features), jnp.float32)
    solved = jnp.zeros((total_rows, features), jnp.float32)
    parent_base = jnp.where(section_index == 0, above_piece(above_rows, 0), empty_half)
    parent_side = jnp.where(section_index == 0, above_piece(above_rows, 0), empty_half)

    def joint_turn(step_index, state_tuple):
        incoming, parent_base, parent_side, kept_w, solved = state_tuple
        incoming, kept_w = forward_step(step_index, incoming, kept_w)
        parent_base, parent_side, solved = backward_step(
            step_index - (levels - 1), parent_base, parent_side, kept_w, solved
        )
        return (incoming, parent_base, parent_side, kept_w, solved)

    state_tuple = lax.fori_loop(
        0, pieces + 2 * levels - 2, joint_turn, (incoming, parent_base, parent_side, kept_w, solved)
    )
    solved = state_tuple[4]
    return solved[None, None]


def solution(mesh):
    placed = (
        P("section", "scen", None, None),
        P("section", "scen", None, None),
        P("section", "scen", None, None),
        P("section", "scen", None, None),
        P("section", "scen", None, None),
        P("section", "scen", None),
        P(),
        P("scen", None, None),
    )
    return jax.shard_map(
        local,
        mesh=mesh,
        in_specs=placed,
        out_specs=P("section", "scen", None, None),
        check_vma=False,
    )
```

profile of v0, /device:TPU:7, one launch (start us, length us, event | category | flops | bytes accessed | tf_op | source)
XLA Modules:
  0.0 369.5 jit_solution(13995153939010594946)
XLA Ops:
  28.0 341.4 %while.30 = (s32[]{:T(128)}, f32[64,1024]{1,0:T(8,128)S(1)}, bf16[64,1024]{1,0:T(8,128)(2,1)S(1)}, f32[512,1024]{1,0:T(8,128)}, f32[512,1024]{1,0:T(8,128)}, /*i...) while((s32[]{:T(128)}, f32[64,1024]{1,0:T(8,128)S(1)}, ...), condition=%wide.region_7.8_spmd.clone, body=%wide.region_0.7_spmd.clone.sunk | while | flops 537919488 | bytes 14032813 | solution.py:147
  28.1 5.5 %conditional.7 = (bf16[64,1024]{1,0:T(8,128)(2,1)}, f32[512,1024]{1,0:T(8,128)}) conditional(s32[]{:T(128)} %convert_element_type.95, f32[512,1024]{1,0:T(8,128)} %get-tuple-element.821, (s32[]{:T(128)}, s32[]{:T(128)}, f32[512,1024]{1,0:T(8,128)}, s32[]{:T(128)}, bf16[1024,1024]{1,0:T(8,128)(2,1)S(1)}, /*index=5*/bf16[1024,1024]{1,0:T(8,128)(2,1)}, ...), branch_computations={%region_1.1_spmd, %region_2.4_spmd} | conditional | flops 268828672 | bytes 5641861 | solution.py:91
  37.6 4.3 %collective-permute-start.1 = (bf16[64,1024]{1,0:T(8,128)(2,1)S(1)}, bf16[64,1024]{1,0:T(8,128)(2,1)S(1)}, u32[]{:S(2)}, u32[]{:S(2)}) collective-permute-start(bf16[64,1024]{1,0:T(8,128)(2,1)S(1)} %collective-permute-done), channel_id=1, source_target_pairs={{0,1},{1,2},{2,3},{3,4},{4,5},{5,6},{6,7},{8,9},{9,10},{10,11},{11... | collective-permute-start | bytes 393224 | tf_op jit(solution)/shard_map/while/body/eval_jaxpr/ppermute | solution.py:12
  43.9 4.5 %collective-permute-done.3 = bf16[64,1024]{1,0:T(8,128)(2,1)S(1)} collective-permute-done((bf16[64,1024]{1,0:T(8,128)(2,1)S(1)}, bf16[64,1024]{1,0:T(8,128)(2,1)S(1)}, u32[]{:S(2)}, u32[]{:S(2)}) %collective-permute-start.3) | collective-permute-done | bytes 131104 | tf_op jit(solution)/shard_map/while/body/eval_jaxpr/ppermute | solution.py:12
  49.4 5.5 %conditional.7 = (bf16[64,1024]{1,0:T(8,128)(2,1)}, f32[512,1024]{1,0:T(8,128)}) conditional(s32[]{:T(128)} %convert_element_type.95, f32[512,1024]{1,0:T(8,128)} %get-tuple-element.821, (s32[]{:T(128)}, s32[]{:T(128)}, f32[512,1024]{1,0:T(8,128)}, s32[]{:T(128)}, bf16[1024,1024]{1,0:T(8,128)(2,1)S(1)}, /*index=5*/bf16[1024,1024]{1,0:T(8,128)(2,1)}, ...), branch_computations={%region_1.1_spmd, %region_2.4_spmd} | conditional | flops 268828672 | bytes 5641861 | solution.py:91
  54.9 4.3 %collective-permute-start = (bf16[64,1024]{1,0:T(8,128)(2,1)}, bf16[64,1024]{1,0:T(8,128)(2,1)S(1)}, u32[]{:S(2)}, u32[]{:S(2)}) collective-permute-start(bf16[64,1024]{1,0:T(8,128)(2,1)} %get-tuple-element.781), channel_id=1, source_target_pairs={{8,0},{16,8},{24,16},{9,1},{17,9},{25,17},{10,2},{18,10},{26,18},{... | collective-permute-start | bytes 393224 | tf_op jit(solution)/shard_map/while/body/eval_jaxpr/ppermute | solution.py:12
  62.6 4.3 %collective-permute-start.1 = (bf16[64,1024]{1,0:T(8,128)(2,1)S(1)}, bf16[64,1024]{1,0:T(8,128)(2,1)S(1)}, u32[]{:S(2)}, u32[]{:S(2)}) collective-permute-start(bf16[64,1024]{1,0:T(8,128)(2,1)S(1)} %collective-permute-done), channel_id=1, source_target_pairs={{0,1},{1,2},{2,3},{3,4},{4,5},{5,6},{6,7},{8,9},{9,10},{10,11},{11... | collective-permute-start | bytes 393224 | tf_op jit(solution)/shard_map/while/body/eval_jaxpr/ppermute | solution.py:12
  68.9 4.5 %collective-permute-done.3 = bf16[64,1024]{1,0:T(8,128)(2,1)S(1)} collective-permute-done((bf16[64,1024]{1,0:T(8,128)(2,1)S(1)}, bf16[64,1024]{1,0:T(8,128)(2,1)S(1)}, u32[]{:S(2)}, u32[]{:S(2)}) %collective-permute-start.3) | collective-permute-done | bytes 131104 | tf_op jit(solution)/shard_map/while/body/eval_jaxpr/ppermute | solution.py:12
  74.3 5.5 %conditional.7 = (bf16[64,1024]{1,0:T(8,128)(2,1)}, f32[512,1024]{1,0:T(8,128)}) conditional(s32[]{:T(128)} %convert_element_type.95, f32[512,1024]{1,0:T(8,128)} %get-tuple-element.821, (s32[]{:T(128)}, s32[]{:T(128)}, f32[512,1024]{1,0:T(8,128)}, s32[]{:T(128)}, bf16[1024,1024]{1,0:T(8,128)(2,1)S(1)}, /*index=5*/bf16[1024,1024]{1,0:T(8,128)(2,1)}, ...), branch_computations={%region_1.1_spmd, %region_2.4_spmd} | conditional | flops 268828672 | bytes 5641861 | solution.py:91
  87.2 4.6 %collective-permute-start.1 = (bf16[64,1024]{1,0:T(8,128)(2,1)S(1)}, bf16[64,1024]{1,0:T(8,128)(2,1)S(1)}, u32[]{:S(2)}, u32[]{:S(2)}) collective-permute-start(bf16[64,1024]{1,0:T(8,128)(2,1)S(1)} %collective-permute-done), channel_id=1, source_target_pairs={{0,1},{1,2},{2,3},{3,4},{4,5},{5,6},{6,7},{8,9},{9,10},{10,11},{11... | collective-permute-start | bytes 393224 | tf_op jit(solution)/shard_map/while/body/eval_jaxpr/ppermute | solution.py:12
  93.8 4.5 %collective-permute-done.3 = bf16[64,1024]{1,0:T(8,128)(2,1)S(1)} collective-permute-done((bf16[64,1024]{1,0:T(8,128)(2,1)S(1)}, bf16[64,1024]{1,0:T(8,128)(2,1)S(1)}, u32[]{:S(2)}, u32[]{:S(2)}) %collective-permute-start.3) | collective-permute-done | bytes 131104 | tf_op jit(solution)/shard_map/while/body/eval_jaxpr/ppermute | solution.py:12
  99.3 5.5 %conditional.7 = (bf16[64,1024]{1,0:T(8,128)(2,1)}, f32[512,1024]{1,0:T(8,128)}) conditional(s32[]{:T(128)} %convert_element_type.95, f32[512,1024]{1,0:T(8,128)} %get-tuple-element.821, (s32[]{:T(128)}, s32[]{:T(128)}, f32[512,1024]{1,0:T(8,128)}, s32[]{:T(128)}, bf16[1024,1024]{1,0:T(8,128)(2,1)S(1)}, /*index=5*/bf16[1024,1024]{1,0:T(8,128)(2,1)}, ...), branch_computations={%region_1.1_spmd, %region_2.4_spmd} | conditional | flops 268828672 | bytes 5641861 | solution.py:91
  111.7 4.4 %collective-permute-start.1 = (bf16[64,1024]{1,0:T(8,128)(2,1)S(1)}, bf16[64,1024]{1,0:T(8,128)(2,1)S(1)}, u32[]{:S(2)}, u32[]{:S(2)}) collective-permute-start(bf16[64,1024]{1,0:T(8,128)(2,1)S(1)} %collective-permute-done), channel_id=1, source_target_pairs={{0,1},{1,2},{2,3},{3,4},{4,5},{5,6},{6,7},{8,9},{9,10},{10,11},{11... | collective-permute-start | bytes 393224 | tf_op jit(solution)/shard_map/while/body/eval_jaxpr/ppermute | solution.py:12
  118.1 4.5 %collective-permute-done.3 = bf16[64,1024]{1,0:T(8,128)(2,1)S(1)} collective-permute-done((bf16[64,1024]{1,0:T(8,128)(2,1)S(1)}, bf16[64,1024]{1,0:T(8,128)(2,1)S(1)}, u32[]{:S(2)}, u32[]{:S(2)}) %collective-permute-start.3) | collective-permute-done | bytes 131104 | tf_op jit(solution)/shard_map/while/body/eval_jaxpr/ppermute | solution.py:12
  123.5 5.5 %conditional.7 = (bf16[64,1024]{1,0:T(8,128)(2,1)}, f32[512,1024]{1,0:T(8,128)}) conditional(s32[]{:T(128)} %convert_element_type.95, f32[512,1024]{1,0:T(8,128)} %get-tuple-element.821, (s32[]{:T(128)}, s32[]{:T(128)}, f32[512,1024]{1,0:T(8,128)}, s32[]{:T(128)}, bf16[1024,1024]{1,0:T(8,128)(2,1)S(1)}, /*index=5*/bf16[1024,1024]{1,0:T(8,128)(2,1)}, ...), branch_computations={%region_1.1_spmd, %region_2.4_spmd} | conditional | flops 268828672 | bytes 5641861 | solution.py:91
  129.0 4.3 %collective-permute-start = (bf16[64,1024]{1,0:T(8,128)(2,1)}, bf16[64,1024]{1,0:T(8,128)(2,1)S(1)}, u32[]{:S(2)}, u32[]{:S(2)}) collective-permute-start(bf16[64,1024]{1,0:T(8,128)(2,1)} %get-tuple-element.781), channel_id=1, source_target_pairs={{8,0},{16,8},{24,16},{9,1},{17,9},{25,17},{10,2},{18,10},{26,18},{... | collective-permute-start | bytes 393224 | tf_op jit(solution)/shard_map/while/body/eval_jaxpr/ppermute | solution.py:12
  141.4 5.0 %collective-permute-done.3 = bf16[64,1024]{1,0:T(8,128)(2,1)S(1)} collective-permute-done((bf16[64,1024]{1,0:T(8,128)(2,1)S(1)}, bf16[64,1024]{1,0:T(8,128)(2,1)S(1)}, u32[]{:S(2)}, u32[]{:S(2)}) %collective-permute-start.3) | collective-permute-done | bytes 131104 | tf_op jit(solution)/shard_map/while/body/eval_jaxpr/ppermute | solution.py:12
  147.4 5.5 %conditional.7 = (bf16[64,1024]{1,0:T(8,128)(2,1)}, f32[512,1024]{1,0:T(8,128)}) conditional(s32[]{:T(128)} %convert_element_type.95, f32[512,1024]{1,0:T(8,128)} %get-tuple-element.821, (s32[]{:T(128)}, s32[]{:T(128)}, f32[512,1024]{1,0:T(8,128)}, s32[]{:T(128)}, bf16[1024,1024]{1,0:T(8,128)(2,1)S(1)}, /*index=5*/bf16[1024,1024]{1,0:T(8,128)(2,1)}, ...), branch_computations={%region_1.1_spmd, %region_2.4_spmd} | conditional | flops 268828672 | bytes 5641861 | solution.py:91
  152.9 5.7 %collective-permute-start = (bf16[64,1024]{1,0:T(8,128)(2,1)}, bf16[64,1024]{1,0:T(8,128)(2,1)S(1)}, u32[]{:S(2)}, u32[]{:S(2)}) collective-permute-start(bf16[64,1024]{1,0:T(8,128)(2,1)} %get-tuple-element.781), channel_id=1, source_target_pairs={{8,0},{16,8},{24,16},{9,1},{17,9},{25,17},{10,2},{18,10},{26,18},{... | collective-permute-start | bytes 393224 | tf_op jit(solution)/shard_map/while/body/eval_jaxpr/ppermute | solution.py:12
  166.3 9.1 %collective-permute-done.3 = bf16[64,1024]{1,0:T(8,128)(2,1)S(1)} collective-permute-done((bf16[64,1024]{1,0:T(8,128)(2,1)S(1)}, bf16[64,1024]{1,0:T(8,128)(2,1)S(1)}, u32[]{:S(2)}, u32[]{:S(2)}) %collective-permute-start.3) | collective-permute-done | bytes 131104 | tf_op jit(solution)/shard_map/while/body/eval_jaxpr/ppermute | solution.py:12
  176.4 5.5 %conditional.7 = (bf16[64,1024]{1,0:T(8,128)(2,1)}, f32[512,1024]{1,0:T(8,128)}) conditional(s32[]{:T(128)} %convert_element_type.95, f32[512,1024]{1,0:T(8,128)} %get-tuple-element.821, (s32[]{:T(128)}, s32[]{:T(128)}, f32[512,1024]{1,0:T(8,128)}, s32[]{:T(128)}, bf16[1024,1024]{1,0:T(8,128)(2,1)S(1)}, /*index=5*/bf16[1024,1024]{1,0:T(8,128)(2,1)}, ...), branch_computations={%region_1.1_spmd, %region_2.4_spmd} | conditional | flops 268828672 | bytes 5641861 | solution.py:91
  196.6 5.9 %collective-permute-done.3 = bf16[64,1024]{1,0:T(8,128)(2,1)S(1)} collective-permute-done((bf16[64,1024]{1,0:T(8,128)(2,1)S(1)}, bf16[64,1024]{1,0:T(8,128)(2,1)S(1)}, u32[]{:S(2)}, u32[]{:S(2)}) %collective-permute-start.3) | collective-permute-done | bytes 131104 | tf_op jit(solution)/shard_map/while/body/eval_jaxpr/ppermute | solution.py:12
  203.5 5.5 %conditional.7 = (bf16[64,1024]{1,0:T(8,128)(2,1)}, f32[512,1024]{1,0:T(8,128)}) conditional(s32[]{:T(128)} %convert_element_type.95, f32[512,1024]{1,0:T(8,128)} %get-tuple-element.821, (s32[]{:T(128)}, s32[]{:T(128)}, f32[512,1024]{1,0:T(8,128)}, s32[]{:T(128)}, bf16[1024,1024]{1,0:T(8,128)(2,1)S(1)}, /*index=5*/bf16[1024,1024]{1,0:T(8,128)(2,1)}, ...), branch_computations={%region_1.1_spmd, %region_2.4_spmd} | conditional | flops 268828672 | bytes 5641861 | solution.py:91
  223.9 5.8 %collective-permute-done.3 = bf16[64,1024]{1,0:T(8,128)(2,1)S(1)} collective-permute-done((bf16[64,1024]{1,0:T(8,128)(2,1)S(1)}, bf16[64,1024]{1,0:T(8,128)(2,1)S(1)}, u32[]{:S(2)}, u32[]{:S(2)}) %collective-permute-start.3) | collective-permute-done | bytes 131104 | tf_op jit(solution)/shard_map/while/body/eval_jaxpr/ppermute | solution.py:12
  231.4 7.0 %collective-permute-start = (bf16[64,1024]{1,0:T(8,128)(2,1)}, bf16[64,1024]{1,0:T(8,128)(2,1)S(1)}, u32[]{:S(2)}, u32[]{:S(2)}) collective-permute-start(bf16[64,1024]{1,0:T(8,128)(2,1)} %get-tuple-element.781), channel_id=1, source_target_pairs={{8,0},{16,8},{24,16},{9,1},{17,9},{25,17},{10,2},{18,10},{26,18},{... | collective-permute-start | bytes 393224 | tf_op jit(solution)/shard_map/while/body/eval_jaxpr/ppermute | solution.py:12
  249.2 5.6 %collective-permute-done.3 = bf16[64,1024]{1,0:T(8,128)(2,1)S(1)} collective-permute-done((bf16[64,1024]{1,0:T(8,128)(2,1)S(1)}, bf16[64,1024]{1,0:T(8,128)(2,1)S(1)}, u32[]{:S(2)}, u32[]{:S(2)}) %collective-permute-start.3) | collective-permute-done | bytes 131104 | tf_op jit(solution)/shard_map/while/body/eval_jaxpr/ppermute | solution.py:12
  271.3 10.0 %collective-permute-done.3 = bf16[64,1024]{1,0:T(8,128)(2,1)S(1)} collective-permute-done((bf16[64,1024]{1,0:T(8,128)(2,1)S(1)}, bf16[64,1024]{1,0:T(8,128)(2,1)S(1)}, u32[]{:S(2)}, u32[]{:S(2)}) %collective-permute-start.3) | collective-permute-done | bytes 131104 | tf_op jit(solution)/shard_map/while/body/eval_jaxpr/ppermute | solution.py:12
  283.0 4.6 %collective-permute-start = (bf16[64,1024]{1,0:T(8,128)(2,1)}, bf16[64,1024]{1,0:T(8,128)(2,1)S(1)}, u32[]{:S(2)}, u32[]{:S(2)}) collective-permute-start(bf16[64,1024]{1,0:T(8,128)(2,1)} %get-tuple-element.781), channel_id=1, source_target_pairs={{8,0},{16,8},{24,16},{9,1},{17,9},{25,17},{10,2},{18,10},{26,18},{... | collective-permute-start | bytes 393224 | tf_op jit(solution)/shard_map/while/body/eval_jaxpr/ppermute | solution.py:12
  298.3 5.8 %collective-permute-done.3 = bf16[64,1024]{1,0:T(8,128)(2,1)S(1)} collective-permute-done((bf16[64,1024]{1,0:T(8,128)(2,1)S(1)}, bf16[64,1024]{1,0:T(8,128)(2,1)S(1)}, u32[]{:S(2)}, u32[]{:S(2)}) %collective-permute-start.3) | collective-permute-done | bytes 131104 | tf_op jit(solution)/shard_map/while/body/eval_jaxpr/ppermute | solution.py:12
  318.9 5.6 %collective-permute-done.3 = bf16[64,1024]{1,0:T(8,128)(2,1)S(1)} collective-permute-done((bf16[64,1024]{1,0:T(8,128)(2,1)S(1)}, bf16[64,1024]{1,0:T(8,128)(2,1)S(1)}, u32[]{:S(2)}, u32[]{:S(2)}) %collective-permute-start.3) | collective-permute-done | bytes 131104 | tf_op jit(solution)/shard_map/while/body/eval_jaxpr/ppermute | solution.py:12
  340.9 5.9 %collective-permute-done.3 = bf16[64,1024]{1,0:T(8,128)(2,1)S(1)} collective-permute-done((bf16[64,1024]{1,0:T(8,128)(2,1)S(1)}, bf16[64,1024]{1,0:T(8,128)(2,1)S(1)}, u32[]{:S(2)}, u32[]{:S(2)}) %collective-permute-start.3) | collective-permute-done | bytes 131104 | tf_op jit(solution)/shard_map/while/body/eval_jaxpr/ppermute | solution.py:12
  362.6 6.0 %collective-permute-done.3 = bf16[64,1024]{1,0:T(8,128)(2,1)S(1)} collective-permute-done((bf16[64,1024]{1,0:T(8,128)(2,1)S(1)}, bf16[64,1024]{1,0:T(8,128)(2,1)S(1)}, u32[]{:S(2)}, u32[]{:S(2)}) %collective-permute-start.3) | collective-permute-done | bytes 131104 | tf_op jit(solution)/shard_map/while/body/eval_jaxpr/ppermute | solution.py:12
  (216 shorter events, 292.9 us)
Async XLA Ops:
  34.8 7.1 %collective-permute-start.2 = (bf16[64,1024]{1,0:T(8,128)(2,1)S(1)}, bf16[64,1024]{1,0:T(8,128)(2,1)S(1)}, u32[]{:S(2)}, u32[]{:S(2)}) collective-permute-start(bf16[64,1024]{1,0:T(8,128)(2,1)S(1)} %get-tuple-element.820), channel_id=1, source_target_pairs={{1,0},{2,1},{3,2},{4,3},{5,4},{6,5},{7,6},{9,8},{10,9},{11,10},{12... | collective-permute-start | bytes 393224 | tf_op jit(solution)/shard_map/while/body/eval_jaxpr/ppermute | solution.py:12
  54.9 7.8 %collective-permute-start = (bf16[64,1024]{1,0:T(8,128)(2,1)}, bf16[64,1024]{1,0:T(8,128)(2,1)S(1)}, u32[]{:S(2)}, u32[]{:S(2)}) collective-permute-start(bf16[64,1024]{1,0:T(8,128)(2,1)} %get-tuple-element.781), channel_id=1, source_target_pairs={{8,0},{16,8},{24,16},{9,1},{17,9},{25,17},{10,2},{18,10},{26,18},{... | collective-permute-start | bytes 393224 | tf_op jit(solution)/shard_map/while/body/eval_jaxpr/ppermute | solution.py:12
  59.2 7.7 %collective-permute-start.2 = (bf16[64,1024]{1,0:T(8,128)(2,1)S(1)}, bf16[64,1024]{1,0:T(8,128)(2,1)S(1)}, u32[]{:S(2)}, u32[]{:S(2)}) collective-permute-start(bf16[64,1024]{1,0:T(8,128)(2,1)S(1)} %get-tuple-element.820), channel_id=1, source_target_pairs={{1,0},{2,1},{3,2},{4,3},{5,4},{6,5},{7,6},{9,8},{10,9},{11,10},{12... | collective-permute-start | bytes 393224 | tf_op jit(solution)/shard_map/while/body/eval_jaxpr/ppermute | solution.py:12
  79.8 7.4 %collective-permute-start = (bf16[64,1024]{1,0:T(8,128)(2,1)}, bf16[64,1024]{1,0:T(8,128)(2,1)S(1)}, u32[]{:S(2)}, u32[]{:S(2)}) collective-permute-start(bf16[64,1024]{1,0:T(8,128)(2,1)} %get-tuple-element.781), channel_id=1, source_target_pairs={{8,0},{16,8},{24,16},{9,1},{17,9},{25,17},{10,2},{18,10},{26,18},{... | collective-permute-start | bytes 393224 | tf_op jit(solution)/shard_map/while/body/eval_jaxpr/ppermute | solution.py:12
  84.1 7.8 %collective-permute-start.2 = (bf16[64,1024]{1,0:T(8,128)(2,1)S(1)}, bf16[64,1024]{1,0:T(8,128)(2,1)S(1)}, u32[]{:S(2)}, u32[]{:S(2)}) collective-permute-start(bf16[64,1024]{1,0:T(8,128)(2,1)S(1)} %get-tuple-element.820), channel_id=1, source_target_pairs={{1,0},{2,1},{3,2},{4,3},{5,4},{6,5},{7,6},{9,8},{10,9},{11,10},{12... | collective-permute-start | bytes 393224 | tf_op jit(solution)/shard_map/while/body/eval_jaxpr/ppermute | solution.py:12
  104.8 7.0 %collective-permute-start = (bf16[64,1024]{1,0:T(8,128)(2,1)}, bf16[64,1024]{1,0:T(8,128)(2,1)S(1)}, u32[]{:S(2)}, u32[]{:S(2)}) collective-permute-start(bf16[64,1024]{1,0:T(8,128)(2,1)} %get-tuple-element.781), channel_id=1, source_target_pairs={{8,0},{16,8},{24,16},{9,1},{17,9},{25,17},{10,2},{18,10},{26,18},{... | collective-permute-start | bytes 393224 | tf_op jit(solution)/shard_map/while/body/eval_jaxpr/ppermute | solution.py:12
  109.0 7.1 %collective-permute-start.2 = (bf16[64,1024]{1,0:T(8,128)(2,1)S(1)}, bf16[64,1024]{1,0:T(8,128)(2,1)S(1)}, u32[]{:S(2)}, u32[]{:S(2)}) collective-permute-start(bf16[64,1024]{1,0:T(8,128)(2,1)S(1)} %get-tuple-element.820), channel_id=1, source_target_pairs={{1,0},{2,1},{3,2},{4,3},{5,4},{6,5},{7,6},{9,8},{10,9},{11,10},{12... | collective-permute-start | bytes 393224 | tf_op jit(solution)/shard_map/while/body/eval_jaxpr/ppermute | solution.py:12
  129.0 7.2 %collective-permute-start = (bf16[64,1024]{1,0:T(8,128)(2,1)}, bf16[64,1024]{1,0:T(8,128)(2,1)S(1)}, u32[]{:S(2)}, u32[]{:S(2)}) collective-permute-start(bf16[64,1024]{1,0:T(8,128)(2,1)} %get-tuple-element.781), channel_id=1, source_target_pairs={{8,0},{16,8},{24,16},{9,1},{17,9},{25,17},{10,2},{18,10},{26,18},{... | collective-permute-start | bytes 393224 | tf_op jit(solution)/shard_map/while/body/eval_jaxpr/ppermute | solution.py:12
  152.9 9.2 %collective-permute-start = (bf16[64,1024]{1,0:T(8,128)(2,1)}, bf16[64,1024]{1,0:T(8,128)(2,1)S(1)}, u32[]{:S(2)}, u32[]{:S(2)}) collective-permute-start(bf16[64,1024]{1,0:T(8,128)(2,1)} %get-tuple-element.781), channel_id=1, source_target_pairs={{8,0},{16,8},{24,16},{9,1},{17,9},{25,17},{10,2},{18,10},{26,18},{... | collective-permute-start | bytes 393224 | tf_op jit(solution)/shard_map/while/body/eval_jaxpr/ppermute | solution.py:12
  164.9 10.5 %collective-permute-start.3 = (bf16[64,1024]{1,0:T(8,128)(2,1)S(1)}, bf16[64,1024]{1,0:T(8,128)(2,1)S(1)}, u32[]{:S(2)}, u32[]{:S(2)}) collective-permute-start(bf16[64,1024]{1,0:T(8,128)(2,1)S(1)} %get-tuple-element.783), channel_id=1, source_target_pairs={{0,8},{8,16},{16,24},{1,9},{9,17},{17,25},{2,10},{10,18},{18,26},{... | collective-permute-start | bytes 393224 | tf_op jit(solution)/shard_map/while/body/eval_jaxpr/ppermute | solution.py:12
  181.9 7.1 %collective-permute-start = (bf16[64,1024]{1,0:T(8,128)(2,1)}, bf16[64,1024]{1,0:T(8,128)(2,1)S(1)}, u32[]{:S(2)}, u32[]{:S(2)}) collective-permute-start(bf16[64,1024]{1,0:T(8,128)(2,1)} %get-tuple-element.781), channel_id=1, source_target_pairs={{8,0},{16,8},{24,16},{9,1},{17,9},{25,17},{10,2},{18,10},{26,18},{... | collective-permute-start | bytes 393224 | tf_op jit(solution)/shard_map/while/body/eval_jaxpr/ppermute | solution.py:12
  189.0 7.5 %collective-permute-start.1 = (bf16[64,1024]{1,0:T(8,128)(2,1)S(1)}, bf16[64,1024]{1,0:T(8,128)(2,1)S(1)}, u32[]{:S(2)}, u32[]{:S(2)}) collective-permute-start(bf16[64,1024]{1,0:T(8,128)(2,1)S(1)} %collective-permute-done), channel_id=1, source_target_pairs={{0,1},{1,2},{2,3},{3,4},{4,5},{5,6},{6,7},{8,9},{9,10},{10,11},{11... | collective-permute-start | bytes 393224 | tf_op jit(solution)/shard_map/while/body/eval_jaxpr/ppermute | solution.py:12
  195.3 7.3 %collective-permute-start.3 = (bf16[64,1024]{1,0:T(8,128)(2,1)S(1)}, bf16[64,1024]{1,0:T(8,128)(2,1)S(1)}, u32[]{:S(2)}, u32[]{:S(2)}) collective-permute-start(bf16[64,1024]{1,0:T(8,128)(2,1)S(1)} %get-tuple-element.783), channel_id=1, source_target_pairs={{0,8},{8,16},{16,24},{1,9},{9,17},{17,25},{2,10},{10,18},{18,26},{... | collective-permute-start | bytes 393224 | tf_op jit(solution)/shard_map/while/body/eval_jaxpr/ppermute | solution.py:12
  209.0 7.0 %collective-permute-start = (bf16[64,1024]{1,0:T(8,128)(2,1)}, bf16[64,1024]{1,0:T(8,128)(2,1)S(1)}, u32[]{:S(2)}, u32[]{:S(2)}) collective-permute-start(bf16[64,1024]{1,0:T(8,128)(2,1)} %get-tuple-element.781), channel_id=1, source_target_pairs={{8,0},{16,8},{24,16},{9,1},{17,9},{25,17},{10,2},{18,10},{26,18},{... | collective-permute-start | bytes 393224 | tf_op jit(solution)/shard_map/while/body/eval_jaxpr/ppermute | solution.py:12
  216.0 7.8 %collective-permute-start.1 = (bf16[64,1024]{1,0:T(8,128)(2,1)S(1)}, bf16[64,1024]{1,0:T(8,128)(2,1)S(1)}, u32[]{:S(2)}, u32[]{:S(2)}) collective-permute-start(bf16[64,1024]{1,0:T(8,128)(2,1)S(1)} %collective-permute-done), channel_id=1, source_target_pairs={{0,1},{1,2},{2,3},{3,4},{4,5},{5,6},{6,7},{8,9},{9,10},{10,11},{11... | collective-permute-start | bytes 393224 | tf_op jit(solution)/shard_map/while/body/eval_jaxpr/ppermute | solution.py:12
  222.5 7.2 %collective-permute-start.3 = (bf16[64,1024]{1,0:T(8,128)(2,1)S(1)}, bf16[64,1024]{1,0:T(8,128)(2,1)S(1)}, u32[]{:S(2)}, u32[]{:S(2)}) collective-permute-start(bf16[64,1024]{1,0:T(8,128)(2,1)S(1)} %get-tuple-element.783), channel_id=1, source_target_pairs={{0,8},{8,16},{16,24},{1,9},{9,17},{17,25},{2,10},{10,18},{18,26},{... | collective-permute-start | bytes 393224 | tf_op jit(solution)/shard_map/while/body/eval_jaxpr/ppermute | solution.py:12
  231.4 10.8 %collective-permute-start = (bf16[64,1024]{1,0:T(8,128)(2,1)}, bf16[64,1024]{1,0:T(8,128)(2,1)S(1)}, u32[]{:S(2)}, u32[]{:S(2)}) collective-permute-start(bf16[64,1024]{1,0:T(8,128)(2,1)} %get-tuple-element.781), channel_id=1, source_target_pairs={{8,0},{16,8},{24,16},{9,1},{17,9},{25,17},{10,2},{18,10},{26,18},{... | collective-permute-start | bytes 393224 | tf_op jit(solution)/shard_map/while/body/eval_jaxpr/ppermute | solution.py:12
  242.2 6.9 %collective-permute-start.1 = (bf16[64,1024]{1,0:T(8,128)(2,1)S(1)}, bf16[64,1024]{1,0:T(8,128)(2,1)S(1)}, u32[]{:S(2)}, u32[]{:S(2)}) collective-permute-start(bf16[64,1024]{1,0:T(8,128)(2,1)S(1)} %collective-permute-done), channel_id=1, source_target_pairs={{0,1},{1,2},{2,3},{3,4},{4,5},{5,6},{6,7},{8,9},{9,10},{10,11},{11... | collective-permute-start | bytes 393224 | tf_op jit(solution)/shard_map/while/body/eval_jaxpr/ppermute | solution.py:12
  247.9 6.9 %collective-permute-start.3 = (bf16[64,1024]{1,0:T(8,128)(2,1)S(1)}, bf16[64,1024]{1,0:T(8,128)(2,1)S(1)}, u32[]{:S(2)}, u32[]{:S(2)}) collective-permute-start(bf16[64,1024]{1,0:T(8,128)(2,1)S(1)} %get-tuple-element.783), channel_id=1, source_target_pairs={{0,8},{8,16},{16,24},{1,9},{9,17},{17,25},{2,10},{10,18},{18,26},{... | collective-permute-start | bytes 393224 | tf_op jit(solution)/shard_map/while/body/eval_jaxpr/ppermute | solution.py:12
  256.5 7.4 %collective-permute-start = (bf16[64,1024]{1,0:T(8,128)(2,1)}, bf16[64,1024]{1,0:T(8,128)(2,1)S(1)}, u32[]{:S(2)}, u32[]{:S(2)}) collective-permute-start(bf16[64,1024]{1,0:T(8,128)(2,1)} %get-tuple-element.781), channel_id=1, source_target_pairs={{8,0},{16,8},{24,16},{9,1},{17,9},{25,17},{10,2},{18,10},{26,18},{... | collective-permute-start | bytes 393224 | tf_op jit(solution)/shard_map/while/body/eval_jaxpr/ppermute | solution.py:12
  263.9 7.3 %collective-permute-start.1 = (bf16[64,1024]{1,0:T(8,128)(2,1)S(1)}, bf16[64,1024]{1,0:T(8,128)(2,1)S(1)}, u32[]{:S(2)}, u32[]{:S(2)}) collective-permute-start(bf16[64,1024]{1,0:T(8,128)(2,1)S(1)} %collective-permute-done), channel_id=1, source_target_pairs={{0,1},{1,2},{2,3},{3,4},{4,5},{5,6},{6,7},{8,9},{9,10},{10,11},{11... | collective-permute-start | bytes 393224 | tf_op jit(solution)/shard_map/while/body/eval_jaxpr/ppermute | solution.py:12
  269.9 11.4 %collective-permute-start.3 = (bf16[64,1024]{1,0:T(8,128)(2,1)S(1)}, bf16[64,1024]{1,0:T(8,128)(2,1)S(1)}, u32[]{:S(2)}, u32[]{:S(2)}) collective-permute-start(bf16[64,1024]{1,0:T(8,128)(2,1)S(1)} %get-tuple-element.783), channel_id=1, source_target_pairs={{0,8},{8,16},{16,24},{1,9},{9,17},{17,25},{2,10},{10,18},{18,26},{... | collective-permute-start | bytes 393224 | tf_op jit(solution)/shard_map/while/body/eval_jaxpr/ppermute | solution.py:12
  283.0 7.3 %collective-permute-start = (bf16[64,1024]{1,0:T(8,128)(2,1)}, bf16[64,1024]{1,0:T(8,128)(2,1)S(1)}, u32[]{:S(2)}, u32[]{:S(2)}) collective-permute-start(bf16[64,1024]{1,0:T(8,128)(2,1)} %get-tuple-element.781), channel_id=1, source_target_pairs={{8,0},{16,8},{24,16},{9,1},{17,9},{25,17},{10,2},{18,10},{26,18},{... | collective-permute-start | bytes 393224 | tf_op jit(solution)/shard_map/while/body/eval_jaxpr/ppermute | solution.py:12
  290.3 8.0 %collective-permute-start.1 = (bf16[64,1024]{1,0:T(8,128)(2,1)S(1)}, bf16[64,1024]{1,0:T(8,128)(2,1)S(1)}, u32[]{:S(2)}, u32[]{:S(2)}) collective-permute-start(bf16[64,1024]{1,0:T(8,128)(2,1)S(1)} %collective-permute-done), channel_id=1, source_target_pairs={{0,1},{1,2},{2,3},{3,4},{4,5},{5,6},{6,7},{8,9},{9,10},{10,11},{11... | collective-permute-start | bytes 393224 | tf_op jit(solution)/shard_map/while/body/eval_jaxpr/ppermute | solution.py:12
  297.0 7.2 %collective-permute-start.3 = (bf16[64,1024]{1,0:T(8,128)(2,1)S(1)}, bf16[64,1024]{1,0:T(8,128)(2,1)S(1)}, u32[]{:S(2)}, u32[]{:S(2)}) collective-permute-start(bf16[64,1024]{1,0:T(8,128)(2,1)S(1)} %get-tuple-element.783), channel_id=1, source_target_pairs={{0,8},{8,16},{16,24},{1,9},{9,17},{17,25},{2,10},{10,18},{18,26},{... | collective-permute-start | bytes 393224 | tf_op jit(solution)/shard_map/while/body/eval_jaxpr/ppermute | solution.py:12
  311.9 6.9 %collective-permute-start.1 = (bf16[64,1024]{1,0:T(8,128)(2,1)S(1)}, bf16[64,1024]{1,0:T(8,128)(2,1)S(1)}, u32[]{:S(2)}, u32[]{:S(2)}) collective-permute-start(bf16[64,1024]{1,0:T(8,128)(2,1)S(1)} %collective-permute-done), channel_id=1, source_target_pairs={{0,1},{1,2},{2,3},{3,4},{4,5},{5,6},{6,7},{8,9},{9,10},{10,11},{11... | collective-permute-start | bytes 393224 | tf_op jit(solution)/shard_map/while/body/eval_jaxpr/ppermute | solution.py:12
  317.5 6.9 %collective-permute-start.3 = (bf16[64,1024]{1,0:T(8,128)(2,1)S(1)}, bf16[64,1024]{1,0:T(8,128)(2,1)S(1)}, u32[]{:S(2)}, u32[]{:S(2)}) collective-permute-start(bf16[64,1024]{1,0:T(8,128)(2,1)S(1)} %get-tuple-element.783), channel_id=1, source_target_pairs={{0,8},{8,16},{16,24},{1,9},{9,17},{17,25},{2,10},{10,18},{18,26},{... | collective-permute-start | bytes 393224 | tf_op jit(solution)/shard_map/while/body/eval_jaxpr/ppermute | solution.py:12
  326.2 7.4 %collective-permute-start = (bf16[64,1024]{1,0:T(8,128)(2,1)}, bf16[64,1024]{1,0:T(8,128)(2,1)S(1)}, u32[]{:S(2)}, u32[]{:S(2)}) collective-permute-start(bf16[64,1024]{1,0:T(8,128)(2,1)} %get-tuple-element.781), channel_id=1, source_target_pairs={{8,0},{16,8},{24,16},{9,1},{17,9},{25,17},{10,2},{18,10},{26,18},{... | collective-permute-start | bytes 393224 | tf_op jit(solution)/shard_map/while/body/eval_jaxpr/ppermute | solution.py:12
  333.5 7.3 %collective-permute-start.1 = (bf16[64,1024]{1,0:T(8,128)(2,1)S(1)}, bf16[64,1024]{1,0:T(8,128)(2,1)S(1)}, u32[]{:S(2)}, u32[]{:S(2)}) collective-permute-start(bf16[64,1024]{1,0:T(8,128)(2,1)S(1)} %collective-permute-done), channel_id=1, source_target_pairs={{0,1},{1,2},{2,3},{3,4},{4,5},{5,6},{6,7},{8,9},{9,10},{10,11},{11... | collective-permute-start | bytes 393224 | tf_op jit(solution)/shard_map/while/body/eval_jaxpr/ppermute | solution.py:12
  339.6 7.3 %collective-permute-start.3 = (bf16[64,1024]{1,0:T(8,128)(2,1)S(1)}, bf16[64,1024]{1,0:T(8,128)(2,1)S(1)}, u32[]{:S(2)}, u32[]{:S(2)}) collective-permute-start(bf16[64,1024]{1,0:T(8,128)(2,1)S(1)} %get-tuple-element.783), channel_id=1, source_target_pairs={{0,8},{8,16},{16,24},{1,9},{9,17},{17,25},{2,10},{10,18},{18,26},{... | collective-permute-start | bytes 393224 | tf_op jit(solution)/shard_map/while/body/eval_jaxpr/ppermute | solution.py:12
  355.1 7.3 %collective-permute-start.1 = (bf16[64,1024]{1,0:T(8,128)(2,1)S(1)}, bf16[64,1024]{1,0:T(8,128)(2,1)S(1)}, u32[]{:S(2)}, u32[]{:S(2)}) collective-permute-start(bf16[64,1024]{1,0:T(8,128)(2,1)S(1)} %collective-permute-done), channel_id=1, source_target_pairs={{0,1},{1,2},{2,3},{3,4},{4,5},{5,6},{6,7},{8,9},{9,10},{10,11},{11... | collective-permute-start | bytes 393224 | tf_op jit(solution)/shard_map/while/body/eval_jaxpr/ppermute | solution.py:12
  361.2 7.3 %collective-permute-start.3 = (bf16[64,1024]{1,0:T(8,128)(2,1)S(1)}, bf16[64,1024]{1,0:T(8,128)(2,1)S(1)}, u32[]{:S(2)}, u32[]{:S(2)}) collective-permute-start(bf16[64,1024]{1,0:T(8,128)(2,1)S(1)} %get-tuple-element.783), channel_id=1, source_target_pairs={{0,8},{8,16},{16,24},{1,9},{9,17},{17,25},{2,10},{10,18},{18,26},{... | collective-permute-start | bytes 393224 | tf_op jit(solution)/shard_map/while/body/eval_jaxpr/ppermute | solution.py:12
  (25 other events, 149.5 us)
where the time goes:
time: 373 us; the launch traced here: 369 us
  starting transfers between devices  155 us (42%)
  waiting for transfers between devices  97.4 us (26%)
  matrix products  68.7 us (18%)
  local copies, waits for them, and re-layouts  23.2 us (6%)
  other arithmetic  21 us (6%)
    ppermute x56, starting transfers between devices, shifted(): return lax.ppermute(array, axis, pairs)  155 us
    ppermute x56, waiting for transfers between devices, shifted(): return lax.ppermute(array, axis, pairs)  97.4 us
    dot_general x16, matrix products, times_transposed(): lax.dot_general(left_rows, matrix, (((1,), (1,)), ((), ())), preferred_el...  43.5 us
    dot_general x8, matrix products, backward_compute(): jnp.dot(reduced.astype(jnp.bfloat16), factor, preferred_element_type=jnp....  25.2 us
    unnamed x6, local copies, waits for them, and re-layouts  13.6 us
    select_n x14, other arithmetic, backward_step(): jnp.where(section_index == 0, above_piece(above_rows, step_index + 1), re...  13.1 us
  transfers between devices with their start and end apart: 56, of which 36 were waited for; matrix products, arithmetic and copies ran while one was open for 7% of the time, Pallas kernels for 0%

commit v1 on v0

v1 whole, which is shorter than its diff:
```python
import functools

import jax
import jax.numpy as jnp
from jax import lax
from jax.experimental import pallas as pl
from jax.experimental.pallas import tpu as pltpu
from jax.sharding import PartitionSpec as P

ROWS = 64
LAG = 4
TILE = 256
MESH = pl.DeviceIdType.MESH


def dot_nt(a, b):
    return lax.dot_general(a, b, (((1,), (1,)), ((), ())), preferred_element_type=jnp.float32)


def dot_nn(a, b):
    return lax.dot_general(a, b, (((1,), (0,)), ((), ())), preferred_element_type=jnp.float32)


def kernel(
    levels,
    nodes,
    rows,
    given_ref,
    raw_ref,
    pattern_ref,
    coupling_ref,
    coupling_pattern_ref,
    pivot_ref,
    offsets_ref,
    above_ref,
    out_ref,
    factor,
    link,
    kept,
    up_in,
    up_out,
    side_in,
    side_out,
    dside_in,
    dside_out,
    down_in,
    down_out,
    above_side,
    up_sems,
    side_sems,
    dside_sems,
    down_sems,
    above_sems,
):
    s = lax.axis_index("section")
    j = lax.axis_index("scen")
    total, features = given_ref.shape
    pieces = total // rows
    blocks = pattern_ref.shape[0]
    size = features // blocks
    has_up, has_down = s > 0, s < levels - 1
    has_left, has_right = j > 0, j < nodes - 1
    up_id = {"section": lax.rem(s + levels - 1, levels)}
    down_id = {"section": lax.rem(s + 1, levels)}
    right_id = {"scen": lax.rem(j + 1, nodes)}
    left_id = {"scen": lax.rem(j + nodes - 1, nodes)}

    barrier = pltpu.get_barrier_semaphore()
    count = jnp.int32(0)
    for has, where_to in ((has_up, up_id), (has_down, down_id), (has_left, left_id), (has_right, right_id)):

        @pl.when(has)
        def _(where_to=where_to):
            pl.semaphore_signal(barrier, inc=1, device_id=where_to, device_id_type=MESH)

        count = count + has.astype(jnp.int32)
    pl.semaphore_wait(barrier, count)

    def slot(ref, p):
        return ref.at[pl.ds(pl.multiple_of(p * rows, rows), rows), :]

    def copy(src, dst, sems, p, device):
        return pltpu.make_async_remote_copy(
            src_ref=slot(src, p),
            dst_ref=slot(dst, p),
            send_sem=sems.at[0, p],
            recv_sem=sems.at[1, p],
            device_id=device,
            device_id_type=MESH,
        )

    def up_copy(p):
        return copy(up_out, up_in, up_sems, p, up_id)

    def side_copy(p):
        return copy(side_out, side_in, side_sems, p, right_id)

    def dside_copy(p):
        return copy(dside_out, dside_in, dside_sems, p, left_id)

    def down_copy(p):
        return copy(down_out, down_in, down_sems, p, down_id)

    def above_copy():
        return pltpu.make_async_remote_copy(
            src_ref=above_ref,
            dst_ref=above_side,
            send_sem=above_sems.at[0],
            recv_sem=above_sems.at[1],
            device_id=left_id,
            device_id_type=MESH,
        )

    first = s == 0

    @pl.when(first & has_left)
    def _():
        above_copy().start()

    @pl.when(jnp.logical_not(has_down))
    def _():
        up_in[...] = jnp.zeros_like(up_in)

    @pl.when(jnp.logical_not(has_left))
    def _():
        side_in[...] = jnp.zeros_like(side_in)

    @pl.when(jnp.logical_not(has_right))
    def _():
        dside_in[...] = jnp.zeros_like(dside_in)
        above_side[...] = jnp.zeros_like(above_side)

    spread = (
        lax.broadcasted_iota(jnp.int32, (blocks, features), 1) // size
        == lax.broadcasted_iota(jnp.int32, (blocks, features), 0)
    ).astype(jnp.bfloat16)
    factor_mask = dot_nn(pattern_ref[...].astype(jnp.float32).astype(jnp.bfloat16), spread)
    link_mask = dot_nn(coupling_pattern_ref[...].astype(jnp.float32).astype(jnp.bfloat16), spread)
    col_ids = lax.broadcasted_iota(jnp.int32, (size, features), 1)
    for i in range(blocks):
        part = pl.ds(i * size, size)
        row_ids = lax.broadcasted_iota(jnp.int32, (size, features), 0) + i * size
        keep = (factor_mask[i : i + 1, :] > 0.5) & (row_ids > col_ids)
        unit = jnp.where(row_ids == col_ids, 1.0, 0.0)
        factor[part, :] = jnp.where(keep, raw_ref[part, :].astype(jnp.float32), unit).astype(jnp.bfloat16)
        link[part, :] = jnp.where(
            link_mask[i : i + 1, :] > 0.5, coupling_ref[part, :].astype(jnp.float32), 0.0
        ).astype(jnp.bfloat16)

    own_offset = offsets_ref[s, j]
    left_offset = offsets_ref[s, jnp.maximum(j - 1, 0)]
    child_offset = offsets_ref[jnp.minimum(s + 1, levels - 1), j]
    tile = min(TILE, features)

    def forward(p):
        @pl.when(has_down)
        def _():
            up_copy(p).wait_recv()

        here = pl.ds(pl.multiple_of(p * rows, rows), rows)
        reduced = (given_ref[here, :] - up_in[here, :].astype(jnp.float32)).astype(jnp.bfloat16)
        result = jnp.concatenate(
            [
                dot_nt(reduced[:, : n + tile], factor[n : n + tile, : n + tile])
                for n in range(0, features, tile)
            ],
            axis=1,
        )
        kept[here, :] = result * pivot_ref[...]

        @pl.when(has_up)
        def _():
            side_out[here, :] = dot_nt(result.astype(jnp.bfloat16), link[...]).astype(jnp.bfloat16)

            @pl.when(has_right)
            def _():
                side_copy(p).start()

    def combine(p):
        @pl.when(has_up)
        def _():
            @pl.when(has_left)
            def _():
                side_copy(p).wait_recv()

            here = pl.ds(pl.multiple_of(p * rows, rows), rows)
            own = jnp.where(own_offset == 0, side_out[here, :].astype(jnp.float32), 0.0)
            moved = jnp.where(left_offset == 1, side_in[here, :].astype(jnp.float32), 0.0)
            up_out[here, :] = (own + jnp.where(has_left, moved, 0.0)).astype(jnp.bfloat16)
            up_copy(p).start()

    def backward(p):
        @pl.when(has_up)
        def _():
            down_copy(p).wait_recv()

        here = pl.ds(pl.multiple_of(p * rows, rows), rows)
        reduced = (kept[here, :] - dot_nn(down_in[here, :], link[...])).astype(jnp.bfloat16)
        result = jnp.concatenate(
            [dot_nn(reduced[:, n:], factor[n:, n : n + tile]) for n in range(0, features, tile)], axis=1
        )
        out_ref[here, :] = result

        @pl.when(has_down)
        def _():
            dside_out[here, :] = result.astype(jnp.bfloat16)

            @pl.when(has_left)
            def _():
                dside_copy(p).start()

    def select(p):
        @pl.when(has_down)
        def _():
            @pl.when(has_right)
            def _():
                dside_copy(p).wait_recv()

            here = pl.ds(pl.multiple_of(p * rows, rows), rows)
            down_out[here, :] = jnp.where(
                child_offset == 1,
                dside_in[here, :].astype(jnp.float32),
                dside_out[here, :].astype(jnp.float32),
            ).astype(jnp.bfloat16)
            down_copy(p).start()

    @pl.when(first)
    def _():
        @pl.when(has_right)
        def _():
            above_copy().wait_recv()

        down_in[...] = jnp.where(
            own_offset == 1, above_side[...].astype(jnp.float32), above_ref[...].astype(jnp.float32)
        ).astype(jnp.bfloat16)

    lag = jnp.minimum(LAG * s, pieces)

    def turn(u, carry):
        @pl.when(u < pieces)
        def _():
            forward(u)

        @pl.when((u >= 1) & (u <= pieces))
        def _():
            combine(u - 1)

        v = u - lag

        @pl.when((v >= 0) & (v < pieces))
        def _():
            backward(v)

        @pl.when((v >= 1) & (v <= pieces))
        def _():
            select(v - 1)

        return carry

    lax.fori_loop(0, pieces + lag + 1, turn, 0)

    def finish(p, carry):
        @pl.when(has_up)
        def _():
            up_copy(p).wait_send()

            @pl.when(has_right)
            def _():
                side_copy(p).wait_send()

        @pl.when(has_down)
        def _():
            down_copy(p).wait_send()

            @pl.when(has_left)
            def _():
                dside_copy(p).wait_send()

        return carry

    lax.fori_loop(0, pieces, finish, 0)

    @pl.when(first & has_left)
    def _():
        above_copy().wait_send()


def local(
    right_side,
    inverse_raw,
    inverse_pattern,
    coupling,
    coupling_pattern,
    pivots,
    offsets,
    above_solution,
):
    levels = lax.axis_size("section")
    nodes = lax.axis_size("scen")
    total, features = right_side.shape[2:]
    rows = min(ROWS, total)
    pieces = total // rows
    vmem = pl.BlockSpec(memory_space=pltpu.VMEM)
    half = pltpu.VMEM((total, features), jnp.bfloat16)
    square = pltpu.VMEM((features, features), jnp.bfloat16)
    sems = pltpu.SemaphoreType.DMA((2, pieces))
    solved = pl.pallas_call(
        functools.partial(kernel, levels, nodes, rows),
        out_shape=jax.ShapeDtypeStruct((total, features), jnp.float32),
        in_specs=[vmem] * 6 + [pl.BlockSpec(memory_space=pltpu.SMEM), vmem],
        out_specs=vmem,
        scratch_shapes=[square, square, pltpu.VMEM((total, features), jnp.float32)]
        + [half] * 9
        + [sems] * 4
        + [pltpu.SemaphoreType.DMA((2,))],
        compiler_params=pltpu.CompilerParams(
            collective_id=0, has_side_effects=True, vmem_limit_bytes=60 * 1024 * 1024
        ),
    )(
        right_side[0, 0],
        inverse_raw[0, 0],
        inverse_pattern[0, 0],
        coupling[0, 0],
        coupling_pattern[0, 0],
        pivots[0],
        offsets,
        above_solution[0],
    )
    return solved[None, None]


def solution(mesh):
    placed = (
        P("section", "scen", None, None),
        P("section", "scen", None, None),
        P("section", "scen", None, None),
        P("section", "scen", None, None),
        P("section", "scen", None, None),
        P("section", "scen", None),
        P(),
        P("scen", None, None),
    )
    return jax.shard_map(
        local,
        mesh=mesh,
        in_specs=placed,
        out_specs=P("section", "scen", None, None),
        check_vma=False,
    )
```

time: 373 us -> 98.1 us (0.26)
  starting transfers between devices: 155 us -> 0 us
  waiting for transfers between devices: 97.4 us -> 0 us
  Pallas kernels: 0 us -> 94.8 us
  matrix products: 68.7 us -> 0 us
  other arithmetic: 21 us -> 0 us
  local copies, waits for them, and re-layouts: 23.2 us -> 3.16 us
    ppermute x56 -> x0, starting transfers between devices: 155 us -> none  [shifted(): return lax.ppermute(array, axis, pairs)]
    ppermute x56 -> x0, waiting for transfers between devices: 97.4 us -> none  [shifted(): return lax.ppermute(array, axis, pairs)]
    pallas_call x0 -> x1, Pallas kernels: none -> 94.8 us  [local(): pl.pallas_call(functools.partial(kernel, levels, nodes, rows), out_shape=...]
    dot_general x24 -> x0, matrix products: 68.7 us -> none  [the longest x16 43.5 us: times_transposed(): lax.dot_general(left_rows, matrix, (((1,), (1,)), ((), ())), preferred_el...]
    select_n x17 -> x0, other arithmetic: 19 us -> none  [the longest x14 13.1 us: backward_step(): jnp.where(section_index == 0, above_piece(above_rows, step_index + 1), re...]
    unnamed x6 -> x1, local copies, waits for them, and re-layouts: 13.6 us -> 3.16 us
    broadcast_in_dim x14 -> x0, local copies, waits for them, and re-layouts: 4.29 us -> none  [the longest x12 4.09 us: local(): empty_half = jnp.zeros((piece_rows, features), jnp.bfloat16)]
  transfers between devices with their start and end apart: 56 -> 0, of which waited for: 36 -> 0; matrix products, arithmetic and copies ran while one was open for 7% -> 0% of each run, Pallas kernels for 0% -> 0%
where the time goes in v1:
time: 98.1 us; the launch traced here: 98 us
  Pallas kernels  94.8 us (97%)
  local copies, waits for them, and re-layouts  3.16 us (3%)
    pallas_call x1, Pallas kernels, local(): pl.pallas_call(functools.partial(kernel, levels, nodes, rows), out_shape=...  94.8 us
    unnamed x1, local copies, waits for them, and re-layouts  3.16 us

profile of v1, /device:TPU:7, one launch (start us, length us, event | category | flops | bytes accessed | tf_op | source)
XLA Modules:
  0.0 98.0 jit_solution(2991135735524436228)
XLA Ops:
  0.0 94.8 %shard_map.82 = f32[512,1024]{1,0:T(8,128)} custom-call(f32[512,1024]{1,0:T(8,128)} %bitcast.9, bf16[1024,1024]{1,0:T(8,128)(2,1)} %bitcast.10, s32[16,16]{1,0:T(8,128)} %bitcast.13, bf16[1024,1024]{1,0:T(8,128)(2,1)} %bitcast.11, s32[16,16]{1,0:T(8,128)} %bitcast.14, f32[1,1024]{1,0:T(1,128)} %bitcast.15, s32[4,8]{1,0:T(4,128)} %offsets_ref.1, ...), custom_call_target="tpu_custom_call" | custom-call | tf_op jit(solution)/shard_map/pallas_call | solution.py:307
  94.8 3.2 %copy.10 = f32[1,1,512,1024]{3,2,1,0:T(8,128)} copy(f32[1,1,512,1024]{3,2,1,0:T(8,128)} %bitcast.8) | data formatting | bytes 4194304

commit v2 on v1

--- a/solution.py
+++ b/solution.py
@@ -7,8 +7,8 @@
 from jax.experimental.pallas import tpu as pltpu
 from jax.sharding import PartitionSpec as P
 
-ROWS = 64
-LAG = 4
+ROWS = 32
+LAG = 8
 TILE = 256
 MESH = pl.DeviceIdType.MESH
 
@@ -306,7 +306,7 @@
     sems = pltpu.SemaphoreType.DMA((2, pieces))
     solved = pl.pallas_call(
         functools.partial(kernel, levels, nodes, rows),
-        out_shape=jax.ShapeDtypeStruct((total, features), jnp.float32),
+        out_shape=pltpu.VMEM((total, features), jnp.float32),
         in_specs=[vmem] * 6 + [pl.BlockSpec(memory_space=pltpu.SMEM), vmem],
         out_specs=vmem,
         scratch_shapes=[square, square, pltpu.VMEM((total, features), jnp.float32)]

time: 98.1 us -> 83.2 us (0.85)
  Pallas kernels: 94.8 us -> 81.7 us
  local copies, waits for them, and re-layouts: 3.16 us -> 1.32 us
    pallas_call x1, Pallas kernels: 94.8 us -> 81.7 us  [local(): pl.pallas_call(functools.partial(kernel, levels, nodes, rows), out_shape=...]
    unnamed x1, local copies, waits for them, and re-layouts: 3.16 us -> 1.32 us
where the time goes in v2:
time: 83.2 us; the launch traced here: 83 us
  Pallas kernels  81.7 us (98%)
  local copies, waits for them, and re-layouts  1.32 us (2%)
    pallas_call x1, Pallas kernels, local(): pl.pallas_call(functools.partial(kernel, levels, nodes, rows), out_shape=...  81.7 us

profile of v2, /device:TPU:7, one launch (start us, length us, event | category | flops | bytes accessed | tf_op | source)
XLA Modules:
  0.0 83.0 jit_solution(11982301629884313920)
XLA Ops:
  0.0 81.7 %shard_map.82 = f32[512,1024]{1,0:T(8,128)S(1)} custom-call(f32[512,1024]{1,0:T(8,128)} %bitcast.9, bf16[1024,1024]{1,0:T(8,128)(2,1)} %bitcast.10, s32[16,16]{1,0:T(8,128)} %bitcast.13, bf16[1024,1024]{1,0:T(8,128)(2,1)} %bitcast.11, s32[16,16]{1,0:T(8,128)} %bitcast.14, f32[1,1024]{1,0:T(1,128)} %bitcast.15, s32[4,8]{1,0:T(4,128)} %offsets_ref.1, ...), custom_call_target="tpu_custom_call" | custom-call | tf_op jit(solution)/shard_map/pallas_call | solution.py:307
  81.7 1.3 %copy.10 = f32[1,1,512,1024]{3,2,1,0:T(8,128)} copy(f32[1,1,512,1024]{3,2,1,0:T(8,128)S(1)} %bitcast.8) | data formatting | bytes 4194304

commit v3 on v2

--- a/solution.py
+++ b/solution.py
@@ -11,10 +11,6 @@
 LAG = 8
 TILE = 256
 MESH = pl.DeviceIdType.MESH
-
-
-def dot_nt(a, b):
-    return lax.dot_general(a, b, (((1,), (1,)), ((), ())), preferred_element_type=jnp.float32)
 
 
 def dot_nn(a, b):
@@ -36,6 +32,8 @@
     out_ref,
     factor,
     link,
+    factor_t,
+    link_t,
     kept,
     up_in,
     up_out,
@@ -147,10 +145,16 @@
             link_mask[i : i + 1, :] > 0.5, coupling_ref[part, :].astype(jnp.float32), 0.0
         ).astype(jnp.bfloat16)
 
+    tile = min(TILE, features)
+    for m in range(0, features, tile):
+        for n in range(0, features, tile):
+            if m >= n:
+                factor_t[n : n + tile, m : m + tile] = factor[m : m + tile, n : n + tile].T
+            link_t[n : n + tile, m : m + tile] = link[m : m + tile, n : n + tile].T
+
     own_offset = offsets_ref[s, j]
     left_offset = offsets_ref[s, jnp.maximum(j - 1, 0)]
     child_offset = offsets_ref[jnp.minimum(s + 1, levels - 1), j]
-    tile = min(TILE, features)
 
     def forward(p):
         @pl.when(has_down)
@@ -161,7 +165,7 @@
         reduced = (given_ref[here, :] - up_in[here, :].astype(jnp.float32)).astype(jnp.bfloat16)
         result = jnp.concatenate(
             [
-                dot_nt(reduced[:, : n + tile], factor[n : n + tile, : n + tile])
+                dot_nn(reduced[:, : n + tile], factor_t[: n + tile, n : n + tile])
                 for n in range(0, features, tile)
             ],
             axis=1,
@@ -170,7 +174,7 @@
 
         @pl.when(has_up)
         def _():
-            side_out[here, :] = dot_nt(result.astype(jnp.bfloat16), link[...]).astype(jnp.bfloat16)
+            side_out[here, :] = dot_nn(result.astype(jnp.bfloat16), link_t[...]).astype(jnp.bfloat16)
 
             @pl.when(has_right)
             def _():
@@ -309,7 +313,7 @@
         out_shape=pltpu.VMEM((total, features), jnp.float32),
         in_specs=[vmem] * 6 + [pl.BlockSpec(memory_space=pltpu.SMEM), vmem],
         out_specs=vmem,
-        scratch_shapes=[square, square, pltpu.VMEM((total, features), jnp.float32)]
+        scratch_shapes=[square] * 4 + [pltpu.VMEM((total, features), jnp.float32)]
         + [half] * 9
         + [sems] * 4
         + [pltpu.SemaphoreType.DMA((2,))],

time: 83.2 us -> 82 us (0.986)
  Pallas kernels: 81.7 us -> 80.6 us
    pallas_call x1, Pallas kernels: 81.7 us -> 80.6 us  [local(): pl.pallas_call(functools.partial(kernel, levels, nodes, rows), out_shape=...]
where the time goes in v3:
time: 82 us; the launch traced here: 81.9 us
  Pallas kernels  80.6 us (98%)
  local copies, waits for them, and re-layouts  1.32 us (2%)
    pallas_call x1, Pallas kernels, local(): pl.pallas_call(functools.partial(kernel, levels, nodes, rows), out_shape=...  80.6 us

profile of v3, /device:TPU:7, one launch (start us, length us, event | category | flops | bytes accessed | tf_op | source)
XLA Modules:
  0.0 81.9 jit_solution(13927257645074690652)
XLA Ops:
  0.0 80.6 %shard_map.82 = f32[512,1024]{1,0:T(8,128)S(1)} custom-call(f32[512,1024]{1,0:T(8,128)} %bitcast.9, bf16[1024,1024]{1,0:T(8,128)(2,1)} %bitcast.10, s32[16,16]{1,0:T(8,128)} %bitcast.13, bf16[1024,1024]{1,0:T(8,128)(2,1)} %bitcast.11, s32[16,16]{1,0:T(8,128)} %bitcast.14, f32[1,1024]{1,0:T(1,128)} %bitcast.15, s32[4,8]{1,0:T(4,128)} %offsets_ref.1, ...), custom_call_target="tpu_custom_call" | custom-call | tf_op jit(solution)/shard_map/pallas_call | solution.py:311
  80.6 1.3 %copy.10 = f32[1,1,512,1024]{3,2,1,0:T(8,128)} copy(f32[1,1,512,1024]{3,2,1,0:T(8,128)S(1)} %bitcast.8) | data formatting | bytes 4194304
